TPU v7x, 256 devices: a whole 4x4x8 slice. The times are simulated.
256 devices in a mesh: seq: 64 (over y, z, core), tp: 4 (over x).
Axes of the slice: x: 4, y: 4, z: 8, core: 2. Of those that a mesh axis runs over, the one named last changes fastest.
Arguments:
- short_hidden: bfloat16 [1024, 1280], P('seq', 'tp'), may hold values from -6 to 6
- long_hidden: bfloat16 [4, 1280], P(None, 'tp'), may hold values from -6 to 6
- short_len: int32 [1024], replicated, may hold values from 1 to 127
- short_slot: int32 [1024], replicated, may hold values from 0 to 2047, as said below
- w_query: bfloat16 [1280, 1280], P(None, 'tp'), may hold values from -0.15625 to 0.15625
- w_key: bfloat16 [1280, 1280], P(None, 'tp'), may hold values from -0.15625 to 0.15625
- w_value: bfloat16 [1280, 1280], P(None, 'tp'), may hold values from -0.15625 to 0.15625
- w_out: bfloat16 [1280, 1280], P('tp'), may hold values from -0.15625 to 0.15625
- qk_gain: float32 [1280], P('tp'), may hold values from 0.7 to 2
- step_rate: float32 [1280], replicated, may hold values from 0.1 to 0.6
- short_keys: bfloat16 [2048, 128, 1280], P('seq', None, 'tp'), may hold values from -0.19921875 to 0.19921875
- short_values: bfloat16 [2048, 128, 1280], P('seq', None, 'tp'), may hold values from -6 to 6
- long_keys: bfloat16 [4, 32768, 1280], P(None, 'seq', 'tp'), may hold values from -0.19921875 to 0.19921875
- long_values: bfloat16 [4, 32768, 1280], P(None, 'seq', 'tp'), may hold values from -6 to 6
Outputs:
- short_out: bfloat16 [1024, 1280], P('seq', 'tp')
- long_out: bfloat16 [4, 1280], P(None, 'tp')
Inputs may be any that keep to these rules, and one draw needn't show every extreme that they name: `short_slot`: all slot numbers are distinct; slot s is row s of short_keys and short_values, so it lies on index s // 32 of seq. In every draw some index of seq has all 32 of its slots taken.
All inputs are finite; a program needn't handle non-finite values.
Results may differ from a plain program's by a relative error of at most 0.01.
Values may be sent and summed in bfloat16 or wider, within the bound.
A program may use at most 64 MiB of HBM per device.

v0:
```python
import math

import jax
import jax.numpy as jnp
from jax import lax
from jax.sharding import PartitionSpec as P

HEAD = 64


EPS = 1e-06


def head_unit(x, gain):
    count = x.shape[0]
    parts = x.reshape(count, -1, HEAD)
    parts = parts * lax.rsqrt(jnp.sum(parts * parts, -1, keepdims=True) + EPS)
    return parts.reshape(count, -1) * gain


def row_unit(x):
    return x * lax.rsqrt(jnp.mean(x * x, -1, keepdims=True) + EPS)


def cache_terms(query, keys, values, live):
    batch, positions, width = keys.shape
    key_heads = keys.reshape(batch, positions, width // HEAD, HEAD)
    value_heads = values.reshape(batch, positions, width // HEAD, HEAD)
    query_heads = query.reshape(batch, width // HEAD, HEAD)
    scores = jnp.einsum(
        "bhe,bphe->bhp", query_heads, key_heads, preferred_element_type=jnp.float32
    ) * math.sqrt(HEAD)
    weights = jnp.where(live[:, None, :], jnp.exp(scores), jnp.float32(0.0))
    den = jnp.sum(weights, -1)
    num = jnp.einsum(
        "bhp,bphe->bhe",
        weights.astype(jnp.bfloat16),
        value_heads,
        preferred_element_type=jnp.float32,
    )
    return (num.reshape(batch, width), den)


def on_device(
    short_hidden,
    long_hidden,
    short_len,
    short_slot,
    w_query,
    w_key,
    w_value,
    w_out,
    qk_gain,
    step_rate,
    short_keys,
    short_values,
    long_keys,
    long_values,
):
    full_short, full_long = (
        lax.all_gather(short_hidden, "tp", axis=1, tiled=True),
        lax.all_gather(long_hidden, "tp", axis=1, tiled=True),
    )
    rows = jnp.concatenate([full_short, full_long], 0)
    n_short = full_short.shape[0]
    count = rows.shape[0]
    width = w_query.shape[1]
    head_count = width // HEAD
    q_proj = jnp.dot(rows, w_query, preferred_element_type=jnp.float32)
    k_proj = jnp.dot(rows, w_key, preferred_element_type=jnp.float32)
    v_proj = jnp.dot(rows, w_value, preferred_element_type=jnp.float32)
    query = head_unit(q_proj, qk_gain).astype(jnp.bfloat16)
    new_key = head_unit(k_proj, qk_gain).astype(jnp.bfloat16)
    new_value = v_proj.astype(jnp.bfloat16)
    all_queries = lax.all_gather(query[:n_short], "seq", axis=0, tiled=True)
    total_short = all_queries.shape[0]
    seq_index = lax.axis_index("seq")
    slot_dev = short_keys.shape[0]
    capacity = short_keys.shape[1]
    local_ids = seq_index * slot_dev + jnp.arange(slot_dev, dtype=jnp.int32)
    match = short_slot[None, :] == local_ids[:, None]
    owner = jnp.sum(jnp.where(match, jnp.arange(total_short, dtype=jnp.int32)[None, :], 0), 1)
    filled = jnp.any(match, 1)
    slot_query = jnp.where(
        filled[:, None], jnp.take(all_queries, owner, axis=0), jnp.zeros((), jnp.bfloat16)
    )
    slot_len = jnp.where(filled, jnp.take(short_len, owner, axis=0), 0)
    live = jnp.arange(capacity, dtype=jnp.int32)[None, :] < slot_len[:, None]
    slot_num, slot_den = cache_terms(slot_query, short_keys, short_values, live)
    home_slot = lax.dynamic_slice_in_dim(short_slot, seq_index * n_short, n_short)
    every_num, every_den = (
        lax.all_gather(slot_num.astype(jnp.bfloat16), "seq", axis=0, tiled=True).astype(
            slot_num.dtype
        ),
        lax.all_gather(slot_den.astype(jnp.bfloat16), "seq", axis=0, tiled=True).astype(
            slot_den.dtype
        ),
    )
    short_num = jnp.take(every_num, home_slot, axis=0)
    short_den = jnp.take(every_den, home_slot, axis=0)
    long_count = full_long.shape[0]
    long_live = jnp.ones((long_count, long_keys.shape[1]), dtype=bool)
    long_part_num, long_part_den = cache_terms(query[n_short:], long_keys, long_values, long_live)
    long_num, long_den = lax.psum((long_part_num, long_part_den), "seq")
    cache_num = jnp.concatenate([short_num, long_num], 0).reshape(count, head_count, HEAD)
    cache_den = jnp.concatenate([short_den, long_den], 0)
    query_heads = query.reshape(count, head_count, HEAD)
    key_heads = new_key.reshape(count, head_count, HEAD)
    value_heads = new_value.reshape(count, head_count, HEAD).astype(jnp.float32)
    own = jnp.exp(
        jnp.einsum("rhe,rhe->rh", query_heads, key_heads, preferred_element_type=jnp.float32)
        * math.sqrt(HEAD)
    )
    den = cache_den + own
    num = cache_num + own.astype(jnp.bfloat16).astype(jnp.float32)[..., None] * value_heads
    attended = (num / den[..., None]).reshape(count, width).astype(jnp.bfloat16)
    partial_proj = jnp.dot(attended, w_out, preferred_element_type=jnp.float32)
    tp_index = lax.axis_index("tp")
    proj = lax.psum(partial_proj.astype(jnp.bfloat16), "tp").astype(jnp.float32)
    state = rows.astype(jnp.float32)
    update = state + step_rate * (row_unit(proj) - state)
    result = lax.dynamic_slice_in_dim(row_unit(update), tp_index * width, width, 1)
    result = result.astype(jnp.bfloat16)
    return (result[:n_short], result[n_short:])


def solution(mesh):
    return jax.shard_map(
        on_device,
        mesh=mesh,
        in_specs=(
            P("seq", "tp"),
            P(None, "tp"),
            P(),
            P(),
            P(None, "tp"),
            P(None, "tp"),
            P(None, "tp"),
            P("tp", None),
            P("tp"),
            P(),
            P("seq", None, "tp"),
            P("seq", None, "tp"),
            P(None, "seq", "tp"),
            P(None, "seq", "tp"),
        ),
        out_specs=(P("seq", "tp"), P(None, "tp")),
        check_vma=False,
    )
```

profile of v0, /device:TPU:1, one launch (start us, length us, event | category | flops | bytes accessed | tf_op | source)
XLA Modules:
  0.0 433.8 jit_solution(15223891977575141921)
XLA Ops:
  7.3 1.0 fusion.5
  8.3 0.9 compare_reduce_fusion
  9.2 1.4 gather_fusion
  10.7 10.3 %all-gather.1 = bf16[4,320,4]{1,2,0:T(4,128)(2,1)S(1)} all-gather(bf16[1,320,4]{1,2,0:T(4,128)(2,1)} %bitcast.82), channel_id=1, replica_groups=mesh['seq'=64,'tp'=4] {'tp'}, dimensions={0}, use_global_device_ids=true | all-gather | bytes 12800 | tf_op jit(solution)/shard_map/all_gather | solution.py:62
  21.0 0.1 reshape.188
  21.1 9.2 %all-gather = bf16[4,320,16]{1,2,0:T(8,128)(2,1)S(1)} all-gather(bf16[1,320,16]{1,2,0:T(8,128)(2,1)} %bitcast.80), channel_id=1, replica_groups=mesh['seq'=64,'tp'=4] {'tp'}, dimensions={0}, use_global_device_ids=true | all-gather | bytes 51200 | tf_op jit(solution)/shard_map/all_gather | solution.py:61
  30.4 0.1 reshape.186
  30.5 1.5 fusion.39
  32.0 0.1 reduce_sum.67
  32.3 1.5 fusion.38
  33.9 0.1 reduce_sum.68
  34.2 60.3 %all_gather.17 = bf16[1024,320]{1,0:T(8,128)(2,1)S(1)} all-gather(bf16[16,320]{1,0:T(8,128)(2,1)S(1)} %slice.24), channel_id=1, replica_groups=mesh['seq'=64,'tp'=4] {'seq'}, dimensions={0}, use_global_device_ids=true | all-gather | bytes 665600 | tf_op jit(solution)/shard_map/all_gather | solution.py:75
  94.5 0.6 gather_fusion.1
  95.1 0.1 gather.20
  95.2 0.1 select_bitcast_fusion
  95.4 0.8 fusion.13
  96.2 0.1 fusion.17
  96.3 0.7 copy-done.3
  97.0 1.5 fusion.11
  98.4 0.7 convert_element_type.59
  99.2 0.1 reshape.204
  99.3 1.6 fusion.40
  100.8 0.1 fusion.27
  101.0 1.8 fusion.19
  102.7 0.1 reshape.148
  102.8 243.5 %all-reduce = (f32[4,5]{0,1:T(8,128)S(1)}, f32[4,320]{1,0:T(4,128)S(1)}) all-reduce(f32[4,5]{0,1:T(8,128)S(1)} %get-tuple-element.13, f32[4,320]{1,0:T(4,128)S(1)} %reshape.148), channel_id=1, replica_groups=mesh['seq'=64,'tp'=4] {'seq'}, use_global_device_ids=true, to_apply=%region_7.8 | all-reduce | flops 1300 | bytes 10400 | tf_op jit(solution)/shard_map/psum | solution.py:104
  346.3 0.1 reshape.149
  346.4 0.1 reshape.150
  346.5 0.1 fusion.8
  346.6 0.1 copy.58
  346.7 52.1 %all-gather.2 = bf16[64,32,5]{1,2,0:T(8,128)(2,1)S(1)} all-gather(bf16[1,32,5]{1,2,0:T(8,128)(2,1)S(1)} %bitcast.81), channel_id=1, replica_groups=mesh['seq'=64,'tp'=4] {'seq'}, dimensions={0}, use_global_device_ids=true | all-gather | bytes 20800 | tf_op jit(solution)/shard_map/all_gather | solution.py:95
  398.8 0.1 copy.41
  398.9 1.8 copy.60
  400.7 0.8 compare_and_fusion.1
  401.5 1.8 gather_fusion.3
  403.3 0.1 copy.44
  403.5 0.1 copy.40
  403.6 0.1 copy.45
  403.7 0.1 div.17
  404.0 3.3 convert_element_type.60
  407.3 2.5 gather_fusion.2
  409.9 2.1 convolution_convert_fusion
  412.0 13.3 %psum.23 = bf16[20,1280]{1,0:T(8,128)(2,1)S(1)} all-reduce(bf16[20,1280]{1,0:T(8,128)(2,1)S(1)} %convolution_convert_fusion), channel_id=1, replica_groups=mesh['seq'=64,'tp'=4] {'tp'}, use_global_device_ids=true, to_apply=%region_8.9 | all-reduce | flops 25600 | bytes 102400 | tf_op jit(solution)/shard_map/psum | solution.py:119
  425.4 0.1 fusion.7
  425.5 0.2 multiply_reduce_fusion
  425.7 0.1 fusion.21
  425.8 0.6 slice.27
  426.4 0.6 slice.26
  (39 shorter events, 1.2 us)
Async XLA Ops:
  7.2 88.2 %copy-start = (bf16[32,128,320]{1,2,0:T(8,128)(2,1)S(1)}, bf16[32,128,320]{1,2,0:T(8,128)(2,1)}, u32[]{:S(2)}) copy-start(bf16[32,128,320]{1,2,0:T(8,128)(2,1)} %param.24) | copy-start | bytes 7864324
  7.2 27.0 %copy-start.2 = (f32[320]{0:T(512)S(1)}, f32[320]{0:T(512)}, u32[]{:S(2)}) copy-start(f32[320]{0:T(512)} %param.22) | copy-start | bytes 3844
  7.2 396.8 %all-gather.5.cloned.1.call-start = ((), (), s32[]{:S(2)}) async-start(), calls=%async_computation | async-start | bytes 1597440 | tf_op jit(solution)/shard_map/all_gather | solution.py:92
  95.2 1.7 copy-start.3
  404.0 21.5 %copy-start.1 = (f32[1280]{0:T(1024)S(1)}, f32[1280]{0:T(1024)}, u32[]{:S(2)}) copy-start(f32[1280]{0:T(1024)} %param.23) | copy-start | bytes 15364
Sparse Core Ops, SparseCore 0:
  99.3 73.8 all-gather.4
where the time goes:
time: 437 us; the launch traced here: 434 us
  blocking collectives  389 us (89%)
  between operations  14.3 us (3%)
  local copies, waits for them, and re-layouts  12.7 us (3%)
  matrix products  10.7 us (2%)
  other arithmetic  7.42 us (2%)
    psum x1, blocking collectives, on_device(): long_num, long_den = lax.psum((long_part_num, long_part_den), 'seq')  244 us
    all_gather x1, blocking collectives, on_device(): all_queries = lax.all_gather(query[:n_short], 'seq', axis=0, tiled=True)  60.3 us
    all_gather x1, blocking collectives, on_device(): lax.all_gather(slot_den.astype(jnp.bfloat16), 'seq', axis=0, tiled=True)  52.1 us
    psum x1, blocking collectives, on_device(): proj = lax.psum(partial_proj.astype(jnp.bfloat16), 'tp').astype(jnp.float32)  13.3 us
    all_gather x1, blocking collectives, on_device(): lax.all_gather(long_hidden, 'tp', axis=1, tiled=True)  10.3 us
    all_gather x1, blocking collectives, on_device(): lax.all_gather(short_hidden, 'tp', axis=1, tiled=True)  9.23 us
  transfers between devices with their start and end apart: 1, of which 0 were waited for; matrix products, arithmetic and copies ran while one was open for 2% of the time, Pallas kernels for 0%

commit v1 on v0

v1 whole, which is shorter than its diff:
```python
import functools
import math

import jax
import jax.numpy as jnp
from jax import lax
from jax.experimental import pallas as pl
from jax.experimental.pallas import tpu as pltpu
from jax.sharding import PartitionSpec as P

HEAD = 64
EPS = 1e-06
MESH = pl.DeviceIdType.MESH
F32 = jnp.float32
BF16 = jnp.bfloat16
GRID = {64: (4, 8, 2), 8: (2, 2, 2)}
GROUP = 8
LROWS = 8


def dot(a, b):
    return lax.dot_general(a, b, (((1,), (0,)), ((), ())), preferred_element_type=F32)


def dot_t(a, b):
    return lax.dot_general(a, b, (((1,), (1,)), ((), ())), preferred_element_type=F32)


def lanes(shape):
    return lax.broadcasted_iota(jnp.int32, shape, 1)


def rows_of(shape):
    return lax.broadcasted_iota(jnp.int32, shape, 0)


def head_sums(x):
    head = lanes(x.shape) // HEAD
    return [
        jnp.sum(jnp.where(head == h, x, 0.0), axis=1, keepdims=True)
        for h in range(x.shape[1] // HEAD)
    ]


def spread(columns, shape):
    head = lanes(shape) // HEAD
    out = jnp.broadcast_to(columns[0], shape)
    for h in range(1, len(columns)):
        out = jnp.where(head == h, columns[h], out)
    return out


def head_unit(x, gain):
    scale = [lax.rsqrt(s + EPS) for s in head_sums(x * x)]
    return x * spread(scale, x.shape) * gain


def row_unit(x):
    return x * lax.rsqrt(jnp.sum(x * x, axis=1, keepdims=True) * (1.0 / x.shape[1]) + EPS)


def by_head(q):
    head = lanes(q.shape) // HEAD
    return jnp.concatenate(
        [jnp.where(head == h, q, 0.0) for h in range(q.shape[1] // HEAD)], axis=0
    ).astype(BF16)


def attend(q, keys, values, valid):
    r, width = q.shape
    heads = width // HEAD
    scores = dot(by_head(q), keys)
    weights = jnp.where(jnp.concatenate([valid] * heads, axis=0), jnp.exp(scores), 0.0)
    den = jnp.sum(weights, axis=1, keepdims=True)
    full = dot_t(weights.astype(BF16), values)
    head = lanes((r, width)) // HEAD
    num = full[:r]
    for h in range(1, heads):
        num = jnp.where(head == h, full[h * r : (h + 1) * r], num)
    return num, [den[h * r : (h + 1) * r] for h in range(heads)]


def tail_of(part, columns):
    half = part.shape[1] // 2
    lane = lanes(part.shape)
    out = jnp.where(lane < half, part, 0.0)
    for h, column in enumerate(columns):
        out = jnp.where(lane == half + h, column, out)
    return out


def columns_of(tail, heads):
    half = tail.shape[1] // 2
    lane = lanes(tail.shape)
    return [
        jnp.sum(jnp.where(lane == half + h, tail, 0.0), axis=1, keepdims=True)
        for h in range(heads)
    ]


def side_by_side(ref, lo, hi):
    return jnp.concatenate([ref[i] for i in range(lo, hi)], axis=1)


def far_first(n):
    return sorted(range(1, n), key=lambda d: -min(d, n - d))


def kernel(
    sizes,
    hid_s, hid_l, len_h, slot_h, wq_h, wk_h, wv_h, wo_h, gain_h, rate_h, ks_h, vs_h, kl_h, vl_h,
    out_s, out_l,
    hbuf, hlbuf, len_v, slot_v, wq, wk, wv, wo, gain_v, rate_v, ks, vs, kl, vl,
    sel, sel_t, qz, f2s, f2r, r1s, r1r, r2s, r2r, acc, l1s, l1r, l2s, l2r, x2s, x2r, x3s, x3r,
    lsem, xs_s, xs_r, xl_s, xl_r, f1_s, f1_r, f2_s, f2_rs, l1_s, l1_rs, l2_s, l2_rs,
    r1_s, r1_rs, r2_s, r2_rs, x2_s, x2_rs, x3_s, x3_rs,
):
    ny, nz, nc, nx = sizes
    nw = ny * nc
    ns, width = hid_s.shape
    long_count = hid_l.shape[0]
    depth = wq_h.shape[1]
    heads = width // HEAD
    slot_dev, cap = ks_h.shape[0], ks_h.shape[2]
    total_rows = slot_h.shape[0]
    s = lax.axis_index("seq")
    t = lax.axis_index("tp")
    c = lax.rem(s, nc)
    z = lax.rem(s // nc, nz)
    y = s // (nc * nz)
    w = y * nc + c

    def at(y_, z_, c_, t_):
        return {"seq": (y_ * nz + z_) * nc + c_, "tp": t_}

    x_peer = {d: at(y, z, c, lax.rem(t + d, nx)) for d in far_first(nx)}
    z_peer = {d: at(y, lax.rem(z + d, nz), c, t) for d in far_first(nz)}
    w_at = {d: lax.rem(w + d, nw) for d in far_first(nw)}
    w_peer = {d: at(v // nc, z, lax.rem(v, nc), t) for d, v in w_at.items()}

    barrier = pltpu.get_barrier_semaphore()
    everyone = [*x_peer.values(), *z_peer.values(), *w_peer.values()]
    for peer in everyone:
        pl.semaphore_signal(barrier, inc=1, device_id=peer, device_id_type=MESH)

    local = {}
    for i, (name, src, dst) in enumerate((
        ("hs", hid_s, hbuf.at[t]), ("hl", hid_l, hlbuf.at[t]), ("slot", slot_h, slot_v), ("len", len_h, len_v),
        ("gain", gain_h, gain_v), ("rate", rate_h, rate_v), ("wq", wq_h, wq), ("kl", kl_h, kl), ("vl", vl_h, vl),
        ("wk", wk_h, wk), ("wv", wv_h, wv), ("ks", ks_h, ks), ("vs", vs_h, vs), ("wo", wo_h, wo),
    )):
        local[name] = pltpu.make_async_copy(src, dst, lsem.at[i])
        local[name].start()

    sent = []

    def send(src, dst, s_sem, r_sem, peer):
        copy = pltpu.make_async_remote_copy(
            src_ref=src, dst_ref=dst, send_sem=s_sem, recv_sem=r_sem, device_id=peer, device_id_type=MESH
        )
        copy.start()
        sent.append(copy)
        return copy

    pl.semaphore_wait(barrier, len(everyone))
    x1 = [send(hid_s, hbuf.at[t], xs_s.at[d], xs_r.at[d], p) for d, p in x_peer.items()]
    x1l = [send(hid_l, hlbuf.at[t], xl_s.at[d], xl_r.at[d], p) for d, p in x_peer.items()]

    qz[:, 1 - c] = jnp.zeros((nz, ns, width), BF16)
    local["slot"].wait()
    local["len"].wait()
    span = nz * nc * ns
    per = 128 // (nc * ns)
    ids = rows_of((nw * slot_dev, 128))
    ids = ids // (nc * slot_dev) * (nz * nc * slot_dev) + z * (nc * slot_dev) + lax.rem(ids, nc * slot_dev)
    for i in range(span // 128):
        row = slot_v[pl.ds(y * (span // 128) + i, 1), :]
        hit = jnp.where(ids == row, 1.0, 0.0)
        sel[:, i * 128 : (i + 1) * 128] = hit.astype(BF16)
        sel_t[i * per : (i + 1) * per] = (
            jnp.transpose(hit).astype(BF16).reshape(per, nc, ns, nw * slot_dev)
        )
    mine = rows_of((slot_dev, 128)) + s * slot_dev
    size = jnp.zeros((slot_dev, 128), F32)
    for i in range(total_rows):
        size += jnp.where(mine == slot_v[i : i + 1, :], len_v[i : i + 1, :].astype(F32), 0.0)
    size = jnp.sum(size, axis=1, keepdims=True)

    for name in ("hs", "gain", "wq"):
        local[name].wait()
    for copy in x1:
        copy.wait_recv()
    gain = gain_v[...].reshape(1, width)
    hidden = jnp.concatenate([hbuf[i] for i in range(nx)], axis=1)
    q_short = head_unit(dot_t(hidden, wq[...]), gain).astype(BF16)
    qz[z, c] = q_short
    f1 = [send(qz.at[z, c], qz.at[z, c], f1_s.at[d], f1_r.at[d], p) for d, p in z_peer.items()]

    local["hl"].wait()
    for copy in x1l:
        copy.wait_recv()
    hidden_l = jnp.concatenate([hlbuf[i].astype(F32) for i in range(nx)], axis=1)
    hidden_l = jnp.concatenate([hidden_l, jnp.zeros((LROWS - long_count, depth), F32)], axis=0)
    q_long = head_unit(dot_t(hidden_l.astype(BF16), wq[...]), gain).astype(BF16)
    local["kl"].wait()
    local["vl"].wait()
    positions = kl.shape[0] * kl.shape[2]
    valid = lanes((LROWS, positions)) // kl.shape[2] == rows_of((LROWS, positions))
    num, den = attend(
        q_long.astype(F32) * math.sqrt(HEAD),
        side_by_side(kl, 0, long_count),
        side_by_side(vl, 0, long_count),
        valid,
    )
    l1s[:, :width] = num
    l1s[:, width - 64 :] = tail_of(l1s[:, width - 64 :], den)
    l1r[z] = l1s[...]
    l1 = [send(l1s, l1r.at[z], l1_s.at[d], l1_rs.at[d], p) for d, p in z_peer.items()]

    local["wk"].wait()
    local["wv"].wait()
    state = jnp.concatenate([hidden.astype(F32), hidden_l], axis=0)
    every = state.astype(BF16)
    query = jnp.concatenate([q_short.astype(F32), q_long.astype(F32)], axis=0)
    new_key = head_unit(dot_t(every, wk[...]), gain).astype(BF16).astype(F32)
    new_value = dot_t(every, wv[...]).astype(BF16).astype(F32)
    own = [jnp.exp(v * math.sqrt(HEAD)) for v in head_sums(query * new_key)]
    own_value = spread([v.astype(BF16).astype(F32) for v in own], new_value.shape) * new_value

    for copy in f1:
        copy.wait_recv()
    picked = dot(sel[...], qz[...].reshape(span, width)).astype(BF16)
    f2s[...] = picked.reshape(nw, slot_dev, width)
    f2 = [send(f2s.at[v], f2r.at[w], f2_s.at[d], f2_rs.at[d], w_peer[d]) for d, v in w_at.items()]
    f2r[w] = f2s[w]

    for copy in l1:
        copy.wait_recv()
    l2s[...] = jnp.sum(l1r[...], axis=0)
    l2r[w] = l2s[...]
    l2 = [send(l2s, l2r.at[w], l2_s.at[d], l2_rs.at[d], p) for d, p in w_peer.items()]

    local["ks"].wait()
    local["vs"].wait()
    for copy in f2:
        copy.wait_recv()
    q_slot = jnp.sum(f2r[...].astype(F32), axis=0) * math.sqrt(HEAD)
    reach = GROUP * cap
    place = lanes((GROUP, reach))
    for g in range(slot_dev // GROUP):
        part = slice(g * GROUP, (g + 1) * GROUP)
        inside = place - rows_of((GROUP, reach)) * cap
        valid = jnp.logical_and(inside >= 0, inside < size[part].astype(jnp.int32))
        num, den = attend(
            q_slot[part],
            side_by_side(ks, g * GROUP, (g + 1) * GROUP),
            side_by_side(vs, g * GROUP, (g + 1) * GROUP),
            valid,
        )
        acc[part, :width] = num
        acc[part, width - 64 :] = tail_of(acc[part, width - 64 :], den)
    r1s[...] = acc[...].astype(BF16)
    r1 = [send(r1s, r1r.at[w], r1_s.at[d], r1_rs.at[d], p) for d, p in w_peer.items()]
    r1r[w] = r1s[...]

    local["rate"].wait()
    local["wo"].wait()
    rate = rate_v[...].reshape(1, depth)

    def attended(sums, lo, hi):
        own_part = [v[lo:hi] for v in own]
        under = [a + b for a, b in zip(columns_of(sums[:, width - 64 :], heads), own_part, strict=True)]
        return ((sums[:, :width] + own_value[lo:hi]) / spread(under, (hi - lo, width))).astype(BF16)

    def updated(proj, lo, hi):
        update = state[lo:hi] + rate * (row_unit(proj) - state[lo:hi])
        result = row_unit(update)
        return pltpu.roll(result, lax.rem(depth - t * width, depth), 1)[:, :width]

    for copy in l2:
        copy.wait_recv()
    x3s[...] = dot(attended(jnp.sum(l2r[...], axis=0), ns, ns + LROWS), wo[...])
    x3r[t] = x3s[...]
    x3 = [send(x3s, x3r.at[t], x3_s.at[d], x3_rs.at[d], p) for d, p in x_peer.items()]

    for copy in r1:
        copy.wait_recv()
    back = dot(sel_t[:, c].reshape(nz * ns, nw * slot_dev), r1r[...].reshape(nw * slot_dev, width + 64))
    r2s[...] = back.astype(BF16).reshape(nz, ns, width + 64)
    r2 = [
        send(r2s.at[lax.rem(z + d, nz)], r2r.at[z], r2_s.at[d], r2_rs.at[d], p)
        for d, p in z_peer.items()
    ]
    r2r[z] = r2s[z]

    for copy in x3:
        copy.wait_recv()
    out_l[...] = updated(jnp.sum(x3r[...], axis=0), ns, ns + LROWS)[:long_count].astype(BF16)

    for copy in r2:
        copy.wait_recv()
    sums = jnp.sum(r2r[...].astype(F32), axis=0)
    x2s[...] = dot(attended(sums, 0, ns), wo[...]).astype(BF16)
    x2r[t] = x2s[...]
    x2 = [send(x2s, x2r.at[t], x2_s.at[d], x2_rs.at[d], p) for d, p in x_peer.items()]
    for copy in x2:
        copy.wait_recv()
    out_s[...] = updated(jnp.sum(x2r[...].astype(F32), axis=0), 0, ns).astype(BF16)

    for copy in sent:
        copy.wait_send()


def on_device(
    sizes,
    short_hidden, long_hidden, short_len, short_slot, w_query, w_key, w_value, w_out, qk_gain, step_rate,
    short_keys, short_values, long_keys, long_values,
):
    ny, nz, nc, nx = sizes
    nw = ny * nc
    ns, width = short_hidden.shape
    long_count = long_hidden.shape[0]
    depth = w_query.shape[0]
    slot_dev = short_keys.shape[0]
    wide = width + 64
    total = short_slot.shape[0]
    span = nz * nc * ns
    dma = pltpu.SemaphoreType.DMA
    args = (
        short_hidden, long_hidden, short_len.reshape(total // 128, 128), short_slot.reshape(total // 128, 128),
        w_query.T, w_key.T, w_value.T, w_out, qk_gain, step_rate,
        *(a.transpose(0, 2, 1) for a in (short_keys, short_values, long_keys, long_values)),
    )
    vmem = pltpu.VMEM
    scratch = [
        vmem((nx, ns, width), BF16), vmem((nx, long_count, width), BF16),
        *(vmem(a.shape, a.dtype) for a in args[2:]),
        vmem((nw * slot_dev, span), BF16), vmem((nz, nc, ns, nw * slot_dev), BF16),
        vmem((nz, nc, ns, width), BF16),
        vmem((nw, slot_dev, width), BF16), vmem((nw, slot_dev, width), BF16),
        vmem((slot_dev, wide), BF16), vmem((nw, slot_dev, wide), BF16),
        vmem((nz, ns, wide), BF16), vmem((nz, ns, wide), BF16), vmem((slot_dev, wide), F32),
        vmem((LROWS, wide), F32), vmem((nz, LROWS, wide), F32),
        vmem((LROWS, wide), F32), vmem((nw, LROWS, wide), F32),
        vmem((ns, depth), BF16), vmem((nx, ns, depth), BF16),
        vmem((LROWS, depth), F32), vmem((nx, LROWS, depth), F32),
        dma((14,)), dma((nx,)), dma((nx,)), dma((nx,)), dma((nx,)), dma((nz,)), dma((nz,)), dma((nw,)), dma((nw,)),
        dma((nz,)), dma((nz,)), dma((nw,)), dma((nw,)), dma((nw,)), dma((nw,)), dma((nz,)), dma((nz,)),
        dma((nx,)), dma((nx,)), dma((nx,)), dma((nx,)),
    ]
    return pl.pallas_call(
        functools.partial(kernel, sizes),
        out_shape=(
            jax.ShapeDtypeStruct(short_hidden.shape, BF16),
            jax.ShapeDtypeStruct(long_hidden.shape, BF16),
        ),
        in_specs=[pl.BlockSpec(memory_space=pl.ANY)] * len(args),
        out_specs=(pl.BlockSpec(memory_space=vmem), pl.BlockSpec(memory_space=vmem)),
        scratch_shapes=scratch,
        compiler_params=pltpu.CompilerParams(collective_id=0, has_side_effects=True),
    )(*args)


def solution(mesh):
    sizes = (*GRID[mesh.shape["seq"]], mesh.shape["tp"])
    return jax.shard_map(
        functools.partial(on_device, sizes),
        mesh=mesh,
        in_specs=(
            P("seq", "tp"),
            P(None, "tp"),
            P(),
            P(),
            P(None, "tp"),
            P(None, "tp"),
            P(None, "tp"),
            P("tp", None),
            P("tp"),
            P(),
            P("seq", None, "tp"),
            P("seq", None, "tp"),
            P(None, "seq", "tp"),
            P(None, "seq", "tp"),
        ),
        out_specs=(P("seq", "tp"), P(None, "tp")),
        check_vma=False,
    )
```

time: 437 us -> 44 us (0.10)
  blocking collectives: 389 us -> 0 us
  Pallas kernels: 0 us -> 40.6 us
  between operations: 14.3 us -> 0.64 us
  matrix products: 10.7 us -> 0 us
  local copies, waits for them, and re-layouts: 12.7 us -> 2.55 us
  other arithmetic: 7.42 us -> 0 us
    psum x2 -> x0, blocking collectives: 257 us -> none  [the longest x1 244 us: on_device(): long_num, long_den = lax.psum((long_part_num, long_part_den), 'seq')]
    all_gather x4 -> x0, blocking collectives: 132 us -> none  [the longest x1 60.3 us: on_device(): all_queries = lax.all_gather(query[:n_short], 'seq', axis=0, tiled=True)]
    pallas_call x0 -> x1, Pallas kernels: none -> 40.6 us  [on_device(): pl.pallas_call(functools.partial(kernel, sizes), out_shape=(jax.ShapeDtyp...]
    dot_general x7 -> x0, matrix products: 10.7 us -> none  [the longest x2 3.21 us: cache_terms(): jnp.einsum('bhp,bphe->bhe', weights.astype(jnp.bfloat16), value_heads, pr...]
    gather x5 -> x0, local copies, waits for them, and re-layouts: 6.38 us -> none  [the longest x1 2.47 us: on_device(): short_num = jnp.take(every_num, home_slot, axis=0)]
  transfers between devices with their start and end apart: 1 -> 0, of which waited for: 0 -> 0; matrix products, arithmetic and copies ran while one was open for 2% -> 0% of each run, Pallas kernels for 0% -> 0%
where the time goes in v1:
time: 44 us; the launch traced here: 43.8 us
  Pallas kernels  40.6 us (92%)
  local copies, waits for them, and re-layouts  2.55 us (6%)
  between operations  0.64 us (1%)
    pallas_call x1, Pallas kernels, on_device(): pl.pallas_call(functools.partial(kernel, sizes), out_shape=(jax.ShapeDtyp...  40.6 us
    unnamed x2, local copies, waits for them, and re-layouts  2.55 us

profile of v1, /device:TPU:1, one launch (start us, length us, event | category | flops | bytes accessed | tf_op | source)
XLA Modules:
  0.0 43.8 jit_solution(1754588432254996636)
XLA Ops:
  0.6 40.6 %shard_map.149 = (bf16[16,320]{1,0:T(8,128)(2,1)}, bf16[4,320]{1,0:T(4,128)(2,1)}) custom-call(bf16[16,320]{1,0:T(8,128)(2,1)} %hid_s.1, bf16[4,320]{1,0:T(4,128)(2,1)} %hid_l.1, s32[8,128]{1,0:T(8,128)} %bitcast.16, s32[8,128]{1,0:T(8,128)} %bitcast.17, bf16[320,1280]{1,0:T(8,128)(2,1)} %bitcast.13, bf16[320,1280]{1,0:T(8,128)(2,1)} %bitcast.14, ...), custom_call_target="tpu_custom_call" | custom-call | tf_op jit(solution)/shard_map/pallas_call | solution.py:351
  41.2 1.3 %copy.18 = bf16[16,320]{1,0:T(8,128)(2,1)} copy(bf16[16,320]{1,0:T(8,128)(2,1)} %get-tuple-element.4) | data formatting | bytes 20480
  42.5 1.2 %copy.19 = bf16[4,320]{1,0:T(4,128)(2,1)} copy(bf16[4,320]{1,0:T(4,128)(2,1)} %get-tuple-element.5) | data formatting | bytes 5120

commit v2 on v1

--- a/solution.py
+++ b/solution.py
@@ -110,10 +110,9 @@
     sizes,
     hid_s, hid_l, len_h, slot_h, wq_h, wk_h, wv_h, wo_h, gain_h, rate_h, ks_h, vs_h, kl_h, vl_h,
     out_s, out_l,
-    hbuf, hlbuf, len_v, slot_v, wq, wk, wv, wo, gain_v, rate_v, ks, vs, kl, vl,
+    hbuf, hlbuf, index_v, wq, wkv, wo, gain_v, rate_v, cache_v, long_v,
     sel, sel_t, qz, f2s, f2r, r1s, r1r, r2s, r2r, acc, l1s, l1r, l2s, l2r, x2s, x2r, x3s, x3r,
-    lsem, xs_s, xs_r, xl_s, xl_r, f1_s, f1_r, f2_s, f2_rs, l1_s, l1_rs, l2_s, l2_rs,
-    r1_s, r1_rs, r2_s, r2_rs, x2_s, x2_rs, x3_s, x3_rs,
+    local_sem, send_sem, recv_sem,
 ):
     ny, nz, nc, nx = sizes
     nw = ny * nc
@@ -144,31 +143,36 @@
         pl.semaphore_signal(barrier, inc=1, device_id=peer, device_id_type=MESH)
 
     local = {}
-    for i, (name, src, dst) in enumerate((
-        ("hs", hid_s, hbuf.at[t]), ("hl", hid_l, hlbuf.at[t]), ("slot", slot_h, slot_v), ("len", len_h, len_v),
-        ("gain", gain_h, gain_v), ("rate", rate_h, rate_v), ("wq", wq_h, wq), ("kl", kl_h, kl), ("vl", vl_h, vl),
-        ("wk", wk_h, wk), ("wv", wv_h, wv), ("ks", ks_h, ks), ("vs", vs_h, vs), ("wo", wo_h, wo),
+    for i, (name, dst, *srcs) in enumerate((
+        ("hs", hbuf.at[t], hid_s), ("index", index_v, slot_h, len_h), ("gain", gain_v, gain_h), ("wq", wq, wq_h),
+        ("hl", hlbuf.at[t], hid_l), ("long", long_v, kl_h, vl_h), ("wkv", wkv, wk_h, wv_h), ("cache", cache_v, ks_h, vs_h),
+        ("wo", wo, wo_h), ("rate", rate_v, rate_h),
     )):
-        local[name] = pltpu.make_async_copy(src, dst, lsem.at[i])
-        local[name].start()
+        for k, src in enumerate(srcs):
+            pltpu.make_async_copy(src, dst.at[k] if len(srcs) > 1 else dst, local_sem.at[i]).start()
+        local[name] = pltpu.make_async_copy(dst, dst, local_sem.at[i])
+    kl, vl = long_v.at[0], long_v.at[1]
+    ks, vs = cache_v.at[0], cache_v.at[1]
+    slot_v, len_v = index_v.at[0], index_v.at[1]
 
     sent = []
 
-    def send(src, dst, s_sem, r_sem, peer):
-        copy = pltpu.make_async_remote_copy(
-            src_ref=src, dst_ref=dst, send_sem=s_sem, recv_sem=r_sem, device_id=peer, device_id_type=MESH
-        )
-        copy.start()
-        sent.append(copy)
-        return copy
+    def stage(blocks, copies):
+        k = len(sent)
+        for src, dst, peer in copies:
+            pltpu.make_async_remote_copy(
+                src_ref=src, dst_ref=dst, send_sem=send_sem.at[k], recv_sem=recv_sem.at[k],
+                device_id=peer, device_id_type=MESH,
+            ).start()
+        sent.append(pltpu.make_async_copy(blocks, blocks, send_sem.at[k]))
+        return pltpu.make_async_copy(blocks, blocks, recv_sem.at[k])
 
     pl.semaphore_wait(barrier, len(everyone))
-    x1 = [send(hid_s, hbuf.at[t], xs_s.at[d], xs_r.at[d], p) for d, p in x_peer.items()]
-    x1l = [send(hid_l, hlbuf.at[t], xl_s.at[d], xl_r.at[d], p) for d, p in x_peer.items()]
+    x1 = stage(hbuf.at[: nx - 1], [(hid_s, hbuf.at[t], p) for p in x_peer.values()])
+    x1l = stage(hlbuf.at[: nx - 1], [(hid_l, hlbuf.at[t], p) for p in x_peer.values()])
 
     qz[:, 1 - c] = jnp.zeros((nz, ns, width), BF16)
-    local["slot"].wait()
-    local["len"].wait()
+    local["index"].wait()
     span = nz * nc * ns
     per = 128 // (nc * ns)
     ids = rows_of((nw * slot_dev, 128))
@@ -188,22 +192,19 @@
 
     for name in ("hs", "gain", "wq"):
         local[name].wait()
-    for copy in x1:
-        copy.wait_recv()
+    x1.wait()
     gain = gain_v[...].reshape(1, width)
     hidden = jnp.concatenate([hbuf[i] for i in range(nx)], axis=1)
     q_short = head_unit(dot_t(hidden, wq[...]), gain).astype(BF16)
     qz[z, c] = q_short
-    f1 = [send(qz.at[z, c], qz.at[z, c], f1_s.at[d], f1_r.at[d], p) for d, p in z_peer.items()]
+    f1 = stage(qz.at[: nz - 1, c], [(qz.at[z, c], qz.at[z, c], p) for p in z_peer.values()])
 
     local["hl"].wait()
-    for copy in x1l:
-        copy.wait_recv()
+    x1l.wait()
     hidden_l = jnp.concatenate([hlbuf[i].astype(F32) for i in range(nx)], axis=1)
     hidden_l = jnp.concatenate([hidden_l, jnp.zeros((LROWS - long_count, depth), F32)], axis=0)
     q_long = head_unit(dot_t(hidden_l.astype(BF16), wq[...]), gain).astype(BF16)
-    local["kl"].wait()
-    local["vl"].wait()
+    local["long"].wait()
     positions = kl.shape[0] * kl.shape[2]
     valid = lanes((LROWS, positions)) // kl.shape[2] == rows_of((LROWS, positions))
     num, den = attend(
@@ -214,39 +215,36 @@
     )
     l1s[:, :width] = num
     l1s[:, width - 64 :] = tail_of(l1s[:, width - 64 :], den)
-    l1r[z] = l1s[...]
-    l1 = [send(l1s, l1r.at[z], l1_s.at[d], l1_rs.at[d], p) for d, p in z_peer.items()]
-
-    local["wk"].wait()
-    local["wv"].wait()
+    l1r[w] = l1s[...]
+    l1 = stage(l1r.at[: nw - 1], [(l1s, l1r.at[w], p) for p in w_peer.values()])
+
+    local["wkv"].wait()
     state = jnp.concatenate([hidden.astype(F32), hidden_l], axis=0)
     every = state.astype(BF16)
     query = jnp.concatenate([q_short.astype(F32), q_long.astype(F32)], axis=0)
-    new_key = head_unit(dot_t(every, wk[...]), gain).astype(BF16).astype(F32)
-    new_value = dot_t(every, wv[...]).astype(BF16).astype(F32)
+    new_key = head_unit(dot_t(every, wkv[0]), gain).astype(BF16).astype(F32)
+    new_value = dot_t(every, wkv[1]).astype(BF16).astype(F32)
     own = [jnp.exp(v * math.sqrt(HEAD)) for v in head_sums(query * new_key)]
     own_value = spread([v.astype(BF16).astype(F32) for v in own], new_value.shape) * new_value
 
-    for copy in f1:
-        copy.wait_recv()
+    f1.wait()
     picked = dot(sel[...], qz[...].reshape(span, width)).astype(BF16)
     f2s[...] = picked.reshape(nw, slot_dev, width)
-    f2 = [send(f2s.at[v], f2r.at[w], f2_s.at[d], f2_rs.at[d], w_peer[d]) for d, v in w_at.items()]
+    f2 = stage(f2r.at[: nw - 1], [(f2s.at[v], f2r.at[w], w_peer[d]) for d, v in w_at.items()])
     f2r[w] = f2s[w]
 
-    for copy in l1:
-        copy.wait_recv()
+    l1.wait()
     l2s[...] = jnp.sum(l1r[...], axis=0)
-    l2r[w] = l2s[...]
-    l2 = [send(l2s, l2r.at[w], l2_s.at[d], l2_rs.at[d], p) for d, p in w_peer.items()]
-
-    local["ks"].wait()
-    local["vs"].wait()
-    for copy in f2:
-        copy.wait_recv()
+    l2r[z] = l2s[...]
+    l2 = stage(l2r.at[: nz - 1], [(l2s, l2r.at[z], p) for p in z_peer.values()])
+
+    local["cache"].wait()
+    f2.wait()
     q_slot = jnp.sum(f2r[...].astype(F32), axis=0) * math.sqrt(HEAD)
     reach = GROUP * cap
     place = lanes((GROUP, reach))
+    half = slot_dev // 2
+    r1 = []
     for g in range(slot_dev // GROUP):
         part = slice(g * GROUP, (g + 1) * GROUP)
         inside = place - rows_of((GROUP, reach)) * cap
@@ -259,8 +257,15 @@
         )
         acc[part, :width] = num
         acc[part, width - 64 :] = tail_of(acc[part, width - 64 :], den)
-    r1s[...] = acc[...].astype(BF16)
-    r1 = [send(r1s, r1r.at[w], r1_s.at[d], r1_rs.at[d], p) for d, p in w_peer.items()]
+        if (g + 1) * GROUP % half == 0:
+            done = pl.ds((g + 1) * GROUP - half, half)
+            r1s[done] = acc[done].astype(BF16)
+            r1.append(
+                stage(
+                    r1r.at[: nw - 1, done],
+                    [(r1s.at[done], r1r.at[w, done], p) for p in w_peer.values()],
+                )
+            )
     r1r[w] = r1s[...]
 
     local["rate"].wait()
@@ -277,38 +282,44 @@
         result = row_unit(update)
         return pltpu.roll(result, lax.rem(depth - t * width, depth), 1)[:, :width]
 
-    for copy in l2:
-        copy.wait_recv()
+    l2.wait()
     x3s[...] = dot(attended(jnp.sum(l2r[...], axis=0), ns, ns + LROWS), wo[...])
     x3r[t] = x3s[...]
-    x3 = [send(x3s, x3r.at[t], x3_s.at[d], x3_rs.at[d], p) for d, p in x_peer.items()]
-
-    for copy in r1:
-        copy.wait_recv()
+    x3 = stage(x3r.at[: nx - 1], [(x3s, x3r.at[t], p) for p in x_peer.values()])
+
+    for part in r1:
+        part.wait()
     back = dot(sel_t[:, c].reshape(nz * ns, nw * slot_dev), r1r[...].reshape(nw * slot_dev, width + 64))
     r2s[...] = back.astype(BF16).reshape(nz, ns, width + 64)
-    r2 = [
-        send(r2s.at[lax.rem(z + d, nz)], r2r.at[z], r2_s.at[d], r2_rs.at[d], p)
-        for d, p in z_peer.items()
-    ]
+    r2 = stage(
+        r2r.at[: nz - 1], [(r2s.at[lax.rem(z + d, nz)], r2r.at[z], p) for d, p in z_peer.items()]
+    )
     r2r[z] = r2s[z]
 
-    for copy in x3:
-        copy.wait_recv()
+    x3.wait()
     out_l[...] = updated(jnp.sum(x3r[...], axis=0), ns, ns + LROWS)[:long_count].astype(BF16)
 
-    for copy in r2:
-        copy.wait_recv()
+    r2.wait()
     sums = jnp.sum(r2r[...].astype(F32), axis=0)
     x2s[...] = dot(attended(sums, 0, ns), wo[...]).astype(BF16)
     x2r[t] = x2s[...]
-    x2 = [send(x2s, x2r.at[t], x2_s.at[d], x2_rs.at[d], p) for d, p in x_peer.items()]
-    for copy in x2:
-        copy.wait_recv()
+    x2 = stage(x2r.at[: nx - 1], [(x2s, x2r.at[t], p) for p in x_peer.values()])
+    x2.wait()
     out_s[...] = updated(jnp.sum(x2r[...].astype(F32), axis=0), 0, ns).astype(BF16)
 
-    for copy in sent:
-        copy.wait_send()
+    for part in sent:
+        part.wait()
+
+
+def hand_over(a_s, a_l, out_s, out_l, sem):
+    copies = [
+        pltpu.make_async_copy(a_s, out_s, sem.at[0]),
+        pltpu.make_async_copy(a_l, out_l, sem.at[1]),
+    ]
+    for copy in copies:
+        copy.start()
+    for copy in copies:
+        copy.wait()
 
 
 def on_device(
@@ -334,31 +345,35 @@
     vmem = pltpu.VMEM
     scratch = [
         vmem((nx, ns, width), BF16), vmem((nx, long_count, width), BF16),
-        *(vmem(a.shape, a.dtype) for a in args[2:]),
+        vmem((2, total // 128, 128), jnp.int32), vmem((width, depth), BF16), vmem((2, width, depth), BF16),
+        vmem((width, depth), BF16), vmem((width,), F32), vmem((depth,), F32),
+        vmem((2, *args[10].shape), BF16), vmem((2, *args[12].shape), BF16),
         vmem((nw * slot_dev, span), BF16), vmem((nz, nc, ns, nw * slot_dev), BF16),
         vmem((nz, nc, ns, width), BF16),
         vmem((nw, slot_dev, width), BF16), vmem((nw, slot_dev, width), BF16),
         vmem((slot_dev, wide), BF16), vmem((nw, slot_dev, wide), BF16),
         vmem((nz, ns, wide), BF16), vmem((nz, ns, wide), BF16), vmem((slot_dev, wide), F32),
+        vmem((LROWS, wide), F32), vmem((nw, LROWS, wide), F32),
         vmem((LROWS, wide), F32), vmem((nz, LROWS, wide), F32),
-        vmem((LROWS, wide), F32), vmem((nw, LROWS, wide), F32),
         vmem((ns, depth), BF16), vmem((nx, ns, depth), BF16),
         vmem((LROWS, depth), F32), vmem((nx, LROWS, depth), F32),
-        dma((14,)), dma((nx,)), dma((nx,)), dma((nx,)), dma((nx,)), dma((nz,)), dma((nz,)), dma((nw,)), dma((nw,)),
-        dma((nz,)), dma((nz,)), dma((nw,)), dma((nw,)), dma((nw,)), dma((nw,)), dma((nz,)), dma((nz,)),
-        dma((nx,)), dma((nx,)), dma((nx,)), dma((nx,)),
+        dma((10,)), dma((12,)), dma((12,)),
     ]
-    return pl.pallas_call(
+    results = pl.pallas_call(
         functools.partial(kernel, sizes),
-        out_shape=(
-            jax.ShapeDtypeStruct(short_hidden.shape, BF16),
-            jax.ShapeDtypeStruct(long_hidden.shape, BF16),
-        ),
+        out_shape=(vmem(short_hidden.shape, BF16), vmem(long_hidden.shape, BF16)),
         in_specs=[pl.BlockSpec(memory_space=pl.ANY)] * len(args),
         out_specs=(pl.BlockSpec(memory_space=vmem), pl.BlockSpec(memory_space=vmem)),
         scratch_shapes=scratch,
         compiler_params=pltpu.CompilerParams(collective_id=0, has_side_effects=True),
     )(*args)
+    return pl.pallas_call(
+        hand_over,
+        out_shape=tuple(jax.ShapeDtypeStruct(a.shape, a.dtype) for a in results),
+        in_specs=[pl.BlockSpec(memory_space=vmem)] * 2,
+        out_specs=(pl.BlockSpec(memory_space=pl.ANY), pl.BlockSpec(memory_space=pl.ANY)),
+        scratch_shapes=[dma((2,))],
+    )(*(pltpu.with_memory_space_constraint(a, pltpu.VMEM) for a in results))
 
 
 def solution(mesh):

time: 44 us -> 39.6 us (0.900)
  local copies, waits for them, and re-layouts: 2.55 us -> 0 us
  Pallas kernels: 40.6 us -> 38.3 us
    unnamed x2 -> x0, local copies, waits for them, and re-layouts: 2.55 us -> none
    pallas_call x1 -> x2, Pallas kernels: 40.6 us -> 38.3 us  [the longest x1 37.7 us: on_device(): pl.pallas_call(functools.partial(kernel, sizes), out_shape=(vmem(short_hi...]
where the time goes in v2:
time: 39.6 us; the launch traced here: 38.9 us
  Pallas kernels  38.3 us (97%)
  between operations  0.64 us (2%)
    pallas_call x1, Pallas kernels, on_device(): pl.pallas_call(functools.partial(kernel, sizes), out_shape=(vmem(short_hi...  37.7 us

profile of v2, /device:TPU:1, one launch (start us, length us, event | category | flops | bytes accessed | tf_op | source)
XLA Modules:
  0.0 38.9 jit_solution(4658012881633128571)
XLA Ops:
  0.6 37.7 %shard_map.149 = (bf16[16,320]{1,0:T(8,128)(2,1)S(1)}, bf16[4,320]{1,0:T(4,128)(2,1)S(1)}) custom-call(bf16[16,320]{1,0:T(8,128)(2,1)} %hid_s.1, bf16[4,320]{1,0:T(4,128)(2,1)} %hid_l.1, s32[8,128]{1,0:T(8,128)} %bitcast.16, s32[8,128]{1,0:T(8,128)} %bitcast.17, bf16[320,1280]{1,0:T(8,128)(2,1)} %bitcast.13, bf16[320,1280]{1,0:T(8,128)(2,1)} %bitcast.14, ...), custom_call_target="tpu_custom_call" | custom-call | tf_op jit(solution)/shard_map/pallas_call | solution.py:362
  38.3 0.6 %shard_map.150 = (bf16[16,320]{1,0:T(8,128)(2,1)}, bf16[4,320]{1,0:T(4,128)(2,1)}) custom-call(bf16[16,320]{1,0:T(8,128)(2,1)S(1)} %get-tuple-element.4.a_s, bf16[4,320]{1,0:T(4,128)(2,1)S(1)} %get-tuple-element.5.a_l), custom_call_target="tpu_custom_call" | custom-call | tf_op jit(solution)/shard_map/pallas_call | solution.py:370

commit v3 on v2

--- a/solution.py
+++ b/solution.py
@@ -112,7 +112,7 @@
     out_s, out_l,
     hbuf, hlbuf, index_v, wq, wkv, wo, gain_v, rate_v, cache_v, long_v,
     sel, sel_t, qz, f2s, f2r, r1s, r1r, r2s, r2r, acc, l1s, l1r, l2s, l2r, x2s, x2r, x3s, x3r,
-    local_sem, send_sem, recv_sem,
+    local_sem, send_sem, recv_sem, ready_sem,
 ):
     ny, nz, nc, nx = sizes
     nw = ny * nc
@@ -138,9 +138,21 @@
     w_peer = {d: at(v // nc, z, lax.rem(v, nc), t) for d, v in w_at.items()}
 
     barrier = pltpu.get_barrier_semaphore()
-    everyone = [*x_peer.values(), *z_peer.values(), *w_peer.values()]
-    for peer in everyone:
-        pl.semaphore_signal(barrier, inc=1, device_id=peer, device_id_type=MESH)
+    partner = at(y, z, 1 - c, t)
+
+    def signal(sem, peer):
+        pl.semaphore_signal(sem, inc=1, device_id=peer, device_id_type=MESH)
+
+    for d in far_first(nx):
+        signal(barrier, at(y, z, 0, lax.rem(t + d, nx)))
+    for d in far_first(ny):
+        signal(barrier, at(lax.rem(y + d, ny), z, 0, t))
+    for d in far_first(nz):
+        signal(barrier, at(y, lax.rem(z + d, nz), 1, t))
+
+    @pl.when(c == 1)
+    def _():
+        signal(barrier, partner)
 
     local = {}
     for i, (name, dst, *srcs) in enumerate((
@@ -167,7 +179,15 @@
         sent.append(pltpu.make_async_copy(blocks, blocks, send_sem.at[k]))
         return pltpu.make_async_copy(blocks, blocks, recv_sem.at[k])
 
-    pl.semaphore_wait(barrier, len(everyone))
+    @pl.when(c == 0)
+    def _():
+        pl.semaphore_wait(barrier, nc * (nx - 1 + ny - 1) + 1)
+        signal(ready_sem, partner)
+
+    @pl.when(c == 1)
+    def _():
+        pl.semaphore_wait(ready_sem, 1)
+
     x1 = stage(hbuf.at[: nx - 1], [(hid_s, hbuf.at[t], p) for p in x_peer.values()])
     x1l = stage(hlbuf.at[: nx - 1], [(hid_l, hlbuf.at[t], p) for p in x_peer.values()])
 
@@ -197,6 +217,15 @@
     hidden = jnp.concatenate([hbuf[i] for i in range(nx)], axis=1)
     q_short = head_unit(dot_t(hidden, wq[...]), gain).astype(BF16)
     qz[z, c] = q_short
+    @pl.when(c == 1)
+    def _():
+        pl.semaphore_wait(barrier, nc * (nz - 1))
+        signal(ready_sem, partner)
+
+    @pl.when(c == 0)
+    def _():
+        pl.semaphore_wait(ready_sem, 1)
+
     f1 = stage(qz.at[: nz - 1, c], [(qz.at[z, c], qz.at[z, c], p) for p in z_peer.values()])
 
     local["hl"].wait()
@@ -357,7 +386,7 @@
         vmem((LROWS, wide), F32), vmem((nz, LROWS, wide), F32),
         vmem((ns, depth), BF16), vmem((nx, ns, depth), BF16),
         vmem((LROWS, depth), F32), vmem((nx, LROWS, depth), F32),
-        dma((10,)), dma((12,)), dma((12,)),
+        dma((10,)), dma((12,)), dma((12,)), pltpu.SemaphoreType.REGULAR,
     ]
     results = pl.pallas_call(
         functools.partial(kernel, sizes),

time: 39.6 us -> 38.1 us (0.962); the launches traced: 38.9 us -> 38 us
  Pallas kernels: 38.3 us -> 37.3 us
    pallas_call x1, Pallas kernels: 37.7 us -> 36.7 us  [on_device(): pl.pallas_call(functools.partial(kernel, sizes), out_shape=(vmem(short_hi...]
where the time goes in v3:
time: 38.1 us; the launch traced here: 38 us
  Pallas kernels  37.3 us (98%)
  between operations  0.64 us (2%)
    pallas_call x1, Pallas kernels, on_device(): pl.pallas_call(functools.partial(kernel, sizes), out_shape=(vmem(short_hi...  36.7 us

profile of v3, /device:TPU:1, one launch (start us, length us, event | category | flops | bytes accessed | tf_op | source)
XLA Modules:
  0.0 38.0 jit_solution(2788639268974886538)
XLA Ops:
  0.6 36.7 %shard_map.149 = (bf16[16,320]{1,0:T(8,128)(2,1)S(1)}, bf16[4,320]{1,0:T(4,128)(2,1)S(1)}) custom-call(bf16[16,320]{1,0:T(8,128)(2,1)} %hid_s.1, bf16[4,320]{1,0:T(4,128)(2,1)} %hid_l.1, s32[8,128]{1,0:T(8,128)} %bitcast.16, s32[8,128]{1,0:T(8,128)} %bitcast.17, bf16[320,1280]{1,0:T(8,128)(2,1)} %bitcast.13, bf16[320,1280]{1,0:T(8,128)(2,1)} %bitcast.14, ...), custom_call_target="tpu_custom_call" | custom-call | tf_op jit(solution)/shard_map/pallas_call | solution.py:391
  37.4 0.6 %shard_map.150 = (bf16[16,320]{1,0:T(8,128)(2,1)}, bf16[4,320]{1,0:T(4,128)(2,1)}) custom-call(bf16[16,320]{1,0:T(8,128)(2,1)S(1)} %get-tuple-element.4.a_s, bf16[4,320]{1,0:T(4,128)(2,1)S(1)} %get-tuple-element.5.a_l), custom_call_target="tpu_custom_call" | custom-call | tf_op jit(solution)/shard_map/pallas_call | solution.py:399

commit v4 on v3

--- a/solution.py
+++ b/solution.py
@@ -78,6 +78,64 @@
     for h in range(1, heads):
         num = jnp.where(head == h, full[h * r : (h + 1) * r], num)
     return num, [den[h * r : (h + 1) * r] for h in range(heads)]
+
+
+def attend_slots(query, ks, vs, size, out, lo, hi):
+    width, cap = ks.shape[1], ks.shape[2]
+    main, heads = width - HEAD, width // HEAD
+    reach, groups = GROUP * cap, (hi - lo) // GROUP
+    place = lanes((GROUP, reach)) - rows_of((GROUP, reach)) * cap
+    live, keys_end, values_end, sums, dens = [], [], [], [], []
+    for g in range(groups):
+        first = lo + g * GROUP
+        part = slice(first, first + GROUP)
+        keys, values = (side_by_side(ref, first, first + GROUP) for ref in (ks, vs))
+        keys_end.append(keys[main:])
+        values_end.append(values[main:])
+        live.append(jnp.logical_and(place >= 0, place < size[part].astype(jnp.int32)))
+        scores = dot(by_head(query[part, :main]), keys[:main])
+        mask = jnp.concatenate([live[g]] * (heads - 1), axis=0)
+        weights = jnp.where(mask, jnp.exp(scores), 0.0)
+        dens.append(jnp.sum(weights, axis=1, keepdims=True))
+        full = dot_t(weights.astype(BF16), values[:main])
+        head = lanes((GROUP, main)) // HEAD
+        num = full[:GROUP]
+        for h in range(1, heads - 1):
+            num = jnp.where(head == h, full[h * GROUP : (h + 1) * GROUP], num)
+        sums.append(num)
+    end = jnp.concatenate([query[lo:hi, main:]] * groups, axis=1)
+    end = jnp.where(lanes(end.shape) // HEAD == rows_of(end.shape) // GROUP, end, 0.0).astype(BF16)
+    scores = dot(end, jnp.concatenate(keys_end, axis=0))
+    weights = jnp.where(jnp.concatenate(live, axis=0), jnp.exp(scores), 0.0)
+    den_end = jnp.sum(weights, axis=1, keepdims=True)
+    full = dot_t(weights.astype(BF16), jnp.concatenate(values_end, axis=0))
+    lane = lanes((GROUP, HEAD))
+    rows = []
+    for g in range(groups):
+        part = slice(g * GROUP, (g + 1) * GROUP)
+        columns = [dens[g][h * GROUP : (h + 1) * GROUP] for h in range(heads - 1)] + [den_end[part]]
+        last = jnp.zeros((GROUP, HEAD), F32)
+        for h, column in enumerate(columns):
+            last = jnp.where(lane == h, column, last)
+        rows.append(jnp.concatenate([sums[g], full[part, g * HEAD : (g + 1) * HEAD], last], axis=1))
+    out[lo:hi] = jnp.concatenate(rows, axis=0).astype(BF16)
+
+
+def fold(x):
+    r, width = x.shape
+    whole = width // 128
+    last = x[:, whole * 128 :]
+    parts = [x[:, i * 128 : (i + 1) * 128] for i in range(whole)]
+    parts.append(jnp.concatenate([last[: r // 2], last[r // 2 :]], axis=1))
+    return jnp.concatenate(parts, axis=0).astype(BF16)
+
+
+def unfold(x, r):
+    whole = x.shape[0] // r
+    last = x[whole * r :]
+    parts = [x[i * r : (i + 1) * r] for i in range(whole)]
+    parts.append(jnp.concatenate([last[:, :64], last[:, 64:]], axis=0))
+    return jnp.concatenate(parts, axis=1)
 
 
 def tail_of(part, columns):
@@ -134,7 +192,12 @@
 
     x_peer = {d: at(y, z, c, lax.rem(t + d, nx)) for d in far_first(nx)}
     z_peer = {d: at(y, lax.rem(z + d, nz), c, t) for d in far_first(nz)}
-    w_at = {d: lax.rem(w + d, nw) for d in far_first(nw)}
+    w_at = {
+        (d, e): lax.rem(y + d, ny) * nc + lax.rem(c + e, nc)
+        for d in [*far_first(ny), 0]
+        for e in range(nc)
+        if d or e
+    }
     w_peer = {d: at(v // nc, z, lax.rem(v, nc), t) for d, v in w_at.items()}
 
     barrier = pltpu.get_barrier_semaphore()
@@ -144,13 +207,13 @@
         pl.semaphore_signal(sem, inc=1, device_id=peer, device_id_type=MESH)
 
     for d in far_first(nx):
-        signal(barrier, at(y, z, 0, lax.rem(t + d, nx)))
+        signal(barrier, at(y, z, 1, lax.rem(t + d, nx)))
     for d in far_first(ny):
-        signal(barrier, at(lax.rem(y + d, ny), z, 0, t))
+        signal(barrier, at(lax.rem(y + d, ny), z, 1, t))
     for d in far_first(nz):
-        signal(barrier, at(y, lax.rem(z + d, nz), 1, t))
-
-    @pl.when(c == 1)
+        signal(barrier, at(y, lax.rem(z + d, nz), 0, t))
+
+    @pl.when(c == 0)
     def _():
         signal(barrier, partner)
 
@@ -179,12 +242,12 @@
         sent.append(pltpu.make_async_copy(blocks, blocks, send_sem.at[k]))
         return pltpu.make_async_copy(blocks, blocks, recv_sem.at[k])
 
-    @pl.when(c == 0)
+    @pl.when(c == 1)
     def _():
         pl.semaphore_wait(barrier, nc * (nx - 1 + ny - 1) + 1)
         signal(ready_sem, partner)
 
-    @pl.when(c == 1)
+    @pl.when(c == 0)
     def _():
         pl.semaphore_wait(ready_sem, 1)
 
@@ -210,6 +273,15 @@
         size += jnp.where(mine == slot_v[i : i + 1, :], len_v[i : i + 1, :].astype(F32), 0.0)
     size = jnp.sum(size, axis=1, keepdims=True)
 
+    @pl.when(c == 0)
+    def _():
+        pl.semaphore_wait(barrier, nc * (nz - 1))
+        signal(ready_sem, partner)
+
+    @pl.when(c == 1)
+    def _():
+        pl.semaphore_wait(ready_sem, 1)
+
     for name in ("hs", "gain", "wq"):
         local[name].wait()
     x1.wait()
@@ -217,15 +289,6 @@
     hidden = jnp.concatenate([hbuf[i] for i in range(nx)], axis=1)
     q_short = head_unit(dot_t(hidden, wq[...]), gain).astype(BF16)
     qz[z, c] = q_short
-    @pl.when(c == 1)
-    def _():
-        pl.semaphore_wait(barrier, nc * (nz - 1))
-        signal(ready_sem, partner)
-
-    @pl.when(c == 0)
-    def _():
-        pl.semaphore_wait(ready_sem, 1)
-
     f1 = stage(qz.at[: nz - 1, c], [(qz.at[z, c], qz.at[z, c], p) for p in z_peer.values()])
 
     local["hl"].wait()
@@ -257,8 +320,9 @@
     own_value = spread([v.astype(BF16).astype(F32) for v in own], new_value.shape) * new_value
 
     f1.wait()
-    picked = dot(sel[...], qz[...].reshape(span, width)).astype(BF16)
-    f2s[...] = picked.reshape(nw, slot_dev, width)
+    picked = dot(sel[...], qz[...].reshape(span, width))
+    for u in range(nw):
+        f2s[u] = fold(picked[u * slot_dev : (u + 1) * slot_dev])
     f2 = stage(f2r.at[: nw - 1], [(f2s.at[v], f2r.at[w], w_peer[d]) for d, v in w_at.items()])
     f2r[w] = f2s[w]
 
@@ -269,32 +333,16 @@
 
     local["cache"].wait()
     f2.wait()
-    q_slot = jnp.sum(f2r[...].astype(F32), axis=0) * math.sqrt(HEAD)
-    reach = GROUP * cap
-    place = lanes((GROUP, reach))
+    q_slot = unfold(jnp.sum(f2r[...].astype(F32), axis=0), slot_dev) * math.sqrt(HEAD)
     half = slot_dev // 2
-    r1 = []
-    for g in range(slot_dev // GROUP):
-        part = slice(g * GROUP, (g + 1) * GROUP)
-        inside = place - rows_of((GROUP, reach)) * cap
-        valid = jnp.logical_and(inside >= 0, inside < size[part].astype(jnp.int32))
-        num, den = attend(
-            q_slot[part],
-            side_by_side(ks, g * GROUP, (g + 1) * GROUP),
-            side_by_side(vs, g * GROUP, (g + 1) * GROUP),
-            valid,
+    r1 = [
+        stage(
+            r1r.at[: nw - 1, pl.ds(lo, half)],
+            [(r1s.at[pl.ds(lo, half)], r1r.at[w, pl.ds(lo, half)], p) for p in w_peer.values()],
         )
-        acc[part, :width] = num
-        acc[part, width - 64 :] = tail_of(acc[part, width - 64 :], den)
-        if (g + 1) * GROUP % half == 0:
-            done = pl.ds((g + 1) * GROUP - half, half)
-            r1s[done] = acc[done].astype(BF16)
-            r1.append(
-                stage(
-                    r1r.at[: nw - 1, done],
-                    [(r1s.at[done], r1r.at[w, done], p) for p in w_peer.values()],
-                )
-            )
+        for lo in range(0, slot_dev, half)
+        if attend_slots(q_slot, ks, vs, size, r1s, lo, lo + half) is None
+    ]
     r1r[w] = r1s[...]
 
     local["rate"].wait()
@@ -379,7 +427,7 @@
         vmem((2, *args[10].shape), BF16), vmem((2, *args[12].shape), BF16),
         vmem((nw * slot_dev, span), BF16), vmem((nz, nc, ns, nw * slot_dev), BF16),
         vmem((nz, nc, ns, width), BF16),
-        vmem((nw, slot_dev, width), BF16), vmem((nw, slot_dev, width), BF16),
+        *(vmem((nw, slot_dev // 2 * (width // HEAD), 128), BF16) for _ in range(2)),
         vmem((slot_dev, wide), BF16), vmem((nw, slot_dev, wide), BF16),
         vmem((nz, ns, wide), BF16), vmem((nz, ns, wide), BF16), vmem((slot_dev, wide), F32),
         vmem((LROWS, wide), F32), vmem((nw, LROWS, wide), F32),

time: 38.1 us -> 37.8 us (level)
  no operation moved by 1% of the time
where the time goes in v4:
time: 37.8 us; the launch traced here: 37.7 us
  Pallas kernels  37 us (98%)
  between operations  0.64 us (2%)
    pallas_call x1, Pallas kernels, on_device(): pl.pallas_call(functools.partial(kernel, sizes), out_shape=(vmem(short_hi...  36.4 us

profile of v4, /device:TPU:1, one launch (start us, length us, event | category | flops | bytes accessed | tf_op | source)
XLA Modules:
  0.0 37.7 jit_solution(15540051075712015604)
XLA Ops:
  0.6 36.4 %shard_map.149 = (bf16[16,320]{1,0:T(8,128)(2,1)S(1)}, bf16[4,320]{1,0:T(4,128)(2,1)S(1)}) custom-call(bf16[16,320]{1,0:T(8,128)(2,1)} %hid_s.1, bf16[4,320]{1,0:T(4,128)(2,1)} %hid_l.1, s32[8,128]{1,0:T(8,128)} %bitcast.16, s32[8,128]{1,0:T(8,128)} %bitcast.17, bf16[320,1280]{1,0:T(8,128)(2,1)} %bitcast.13, bf16[320,1280]{1,0:T(8,128)(2,1)} %bitcast.14, ...), custom_call_target="tpu_custom_call" | custom-call | tf_op jit(solution)/shard_map/pallas_call | solution.py:439
  37.0 0.6 %shard_map.150 = (bf16[16,320]{1,0:T(8,128)(2,1)}, bf16[4,320]{1,0:T(4,128)(2,1)}) custom-call(bf16[16,320]{1,0:T(8,128)(2,1)S(1)} %get-tuple-element.4.a_s, bf16[4,320]{1,0:T(4,128)(2,1)S(1)} %get-tuple-element.5.a_l), custom_call_target="tpu_custom_call" | custom-call | tf_op jit(solution)/shard_map/pallas_call | solution.py:447

commit v5 on v4

--- a/solution.py
+++ b/solution.py
@@ -378,10 +378,20 @@
 
     r2.wait()
     sums = jnp.sum(r2r[...].astype(F32), axis=0)
-    x2s[...] = dot(attended(sums, 0, ns), wo[...]).astype(BF16)
+    ready = attended(sums, 0, ns)
+    x2 = []
+    for lo in range(0, depth, depth // 2):
+        cols = pl.ds(lo, depth // 2)
+        x2s[:, cols] = dot(ready, wo[:, cols]).astype(BF16)
+        x2.append(
+            stage(
+                x2r.at[: nx - 1, :, cols],
+                [(x2s.at[:, cols], x2r.at[t, :, cols], p) for p in x_peer.values()],
+            )
+        )
     x2r[t] = x2s[...]
-    x2 = stage(x2r.at[: nx - 1], [(x2s, x2r.at[t], p) for p in x_peer.values()])
-    x2.wait()
+    for part in x2:
+        part.wait()
     out_s[...] = updated(jnp.sum(x2r[...].astype(F32), axis=0), 0, ns).astype(BF16)
 
     for part in sent:

time: 37.8 us -> 37.8 us (level)
  no operation moved by 1% of the time
where the time goes in v5:
time: 37.8 us; the launch traced here: 37.6 us
  Pallas kernels  36.9 us (98%)
  between operations  0.64 us (2%)
    pallas_call x1, Pallas kernels, on_device(): pl.pallas_call(functools.partial(kernel, sizes), out_shape=(vmem(short_hi...  36.3 us

profile of v5, /device:TPU:1, one launch (start us, length us, event | category | flops | bytes accessed | tf_op | source)
XLA Modules:
  0.0 37.6 jit_solution(11695584734274774826)
XLA Ops:
  0.6 36.3 %shard_map.149 = (bf16[16,320]{1,0:T(8,128)(2,1)S(1)}, bf16[4,320]{1,0:T(4,128)(2,1)S(1)}) custom-call(bf16[16,320]{1,0:T(8,128)(2,1)} %hid_s.1, bf16[4,320]{1,0:T(4,128)(2,1)} %hid_l.1, s32[8,128]{1,0:T(8,128)} %bitcast.16, s32[8,128]{1,0:T(8,128)} %bitcast.17, bf16[320,1280]{1,0:T(8,128)(2,1)} %bitcast.13, bf16[320,1280]{1,0:T(8,128)(2,1)} %bitcast.14, ...), custom_call_target="tpu_custom_call" | custom-call | tf_op jit(solution)/shard_map/pallas_call | solution.py:449
  37.0 0.6 %shard_map.150 = (bf16[16,320]{1,0:T(8,128)(2,1)}, bf16[4,320]{1,0:T(4,128)(2,1)}) custom-call(bf16[16,320]{1,0:T(8,128)(2,1)S(1)} %get-tuple-element.4.a_s, bf16[4,320]{1,0:T(4,128)(2,1)S(1)} %get-tuple-element.5.a_l), custom_call_target="tpu_custom_call" | custom-call | tf_op jit(solution)/shard_map/pallas_call | solution.py:457
